TPU v7x, 512 devices: a whole 4x4x16 slice. The times are simulated.
512 devices in a mesh: req: 64 (over y, z), head: 8 (over x, core).
Axes of the slice: x: 4, y: 4, z: 16, core: 2. Of those that a mesh axis runs over, the one named last changes fastest.
Arguments:
- tokens: bfloat16 [256, 2048], P('req'), may hold values from -1.1953125 to 1.1953125
- lengths: int32 [256], replicated, may hold values from 1 to 1021, as said below
- kv_cache: bfloat16 [1, 2, 65536, 8, 128], P(None, None, 'req', 'head'), may hold values from -24 to 24
- w_qkv: bfloat16 [1, 2048, 8, 512], P(None, 'req', 'head'), may hold values from -0.125 to 0.125
- w_headgate: bfloat16 [1, 2048, 16], P(None, None, 'head'), may hold values from -0.125 to 0.125
- w_out: bfloat16 [1, 2048, 2048], P(None, 'head', 'req'), may hold values from -0.5 to 0.5
- in_gain: float32 [1, 2048], replicated, may hold values from 0.5 to 1.5
- q_gain: float32 [1, 128], replicated, may hold values from 0.1 to 1.9
- k_gain: float32 [1, 128], replicated, may hold values from 0.1 to 1.9
- post_gain: float32 [1, 2048], replicated, may hold values from 0.5 to 1.5
- w_gate: bfloat16 [1, 2048, 6144], P(None, 'head', 'req'), may hold values from -0.125 to 0.125
- w_up: bfloat16 [1, 2048, 6144], P(None, 'head', 'req'), may hold values from -0.125 to 0.125
- w_down: bfloat16 [1, 6144, 2048], P(None, 'req', 'head'), may hold values from -0.078125 to 0.078125
- final_gain: float32 [2048], replicated, may hold values from 0.5 to 1.5
- w_vocab: bfloat16 [2048, 131072], P(None, ('req', 'head')), may hold values from -0.125 to 0.125
Outputs:
- logits: bfloat16 [256, 131072], P(None, ('req', 'head'))
Inputs may be any that keep to these rules, and one draw needn't show every extreme that they name: On every index of req the lengths of its 4 requests sum to at most 1024. On 8 indices, drawn anew, they sum to exactly 1024 and one request there is longer than 512; on one of these the other requests hold one token each. On every other index each length is at most 128 and one is exactly 128.
All inputs are finite; a program needn't handle non-finite values.
Results may differ from a plain program's by a relative error of at most 0.015.
Values may be sent and summed in bfloat16 or wider, within the bound.
No kernel may reach another device: no remote copies, remote signals or barrier semaphores. Data moves between devices by JAX's collectives and lax.ppermute only.
A program may use at most 64 MiB of HBM per device.

v0:
```python
import jax
import jax.numpy as jnp
from jax import lax
from jax.sharding import Mesh
from jax.sharding import PartitionSpec as P

EPSILON = 1e-06
ROPE_THETA = 1000000.0
Y, Z, X, C = (4, 16, 4, 2)
ZH, ZL = (4, 4)
DEPTH = ("zh", "zl")
F32, BF16 = (jnp.float32, jnp.bfloat16)


def rms_scale(values, gain):
    mean_square = jnp.mean(values * values, axis=-1, keepdims=True)
    return values * lax.rsqrt(mean_square + EPSILON) * gain


def rotate(values, cosine, sine):
    half = values.shape[-1] // 2
    a, b = (values[..., :half], values[..., half:])
    return jnp.concatenate([a * cosine - b * sine, b * cosine + a * sine], axis=-1)


def swap(values, axes):
    return lax.all_to_all(values, axes, split_axis=0, concat_axis=0, tiled=True)


def spread(values, axes, count):
    return swap(jnp.broadcast_to(values[None], (count,) + values.shape), axes)


def local(
    tokens,
    lengths,
    kv_cache,
    w_qkv,
    w_headgate,
    w_out,
    in_gain,
    q_gain,
    k_gain,
    post_gain,
    w_gate,
    w_up,
    w_down,
    final_gain,
    w_vocab,
):
    rows, width = tokens.shape
    head_dim = q_gain.shape[1]
    columns = w_qkv.shape[3]
    units = w_gate.shape[2]
    seg = width // (X * C)
    part_width = width // C
    req = lax.axis_index(("y",) + DEPTH)
    ix, ic = (lax.axis_index("x"), lax.axis_index("c"))
    ffn = jnp.concatenate([w_gate[0].T, w_up[0].T, w_down[0]], axis=0)
    ffn = lax.all_gather(ffn, ("y", "x"), axis=0).reshape(Y, X, -1, seg)
    qkv_block = lax.all_gather(w_qkv[0, :, 0], "y", axis=0, tiled=True)
    positions = lax.dynamic_slice_in_dim(lengths, req * rows, rows)
    starts = jnp.cumsum(positions) - positions
    limits = starts + positions
    token_wide = tokens.astype(F32)
    gained = (token_wide * in_gain[0]).astype(BF16)
    in_scale = lax.rsqrt(jnp.mean(token_wide * token_wide, axis=-1, keepdims=True) + EPSILON)
    normed = (token_wide * in_scale * in_gain[0]).astype(BF16)
    head_gate = jax.nn.sigmoid(jnp.dot(normed, w_headgate[0], preferred_element_type=F32))
    half = head_dim // 2
    frequency = ROPE_THETA ** (-2.0 * jnp.arange(half, dtype=F32) / head_dim)
    angles = positions.astype(F32)[:, None] * frequency[None, :]
    cosine, sine = (jnp.cos(angles), jnp.sin(angles))

    def own_row(array):
        return lax.dynamic_slice_in_dim(array, ix, 1, 0)

    def own_core(array, axis):
        return lax.dynamic_slice_in_dim(array, ic, 1, axis)

    residual = own_core(own_row(tokens).reshape(Y, C, seg), 1).reshape(8, head_dim)
    slot = jnp.arange(kv_cache.shape[2], dtype=jnp.int32)
    inside = (slot[None, :] >= starts[:, None]) & (slot[None, :] < limits[:, None])
    depth = width // (Y * Z)
    sent = gained.reshape(rows, Y, Z, depth).transpose(2, 0, 1, 3).reshape(Z, rows, Y * depth)
    block = w_out[0].T
    halves = [
        jnp.broadcast_to(
            block[None, :, q * head_dim : (q + 1) * head_dim], (Z, block.shape[0], head_dim)
        )
        for q in (0, 1)
    ]
    sent = jnp.concatenate([sent, jnp.zeros((Z, 8 - rows, head_dim), BF16)] + halves, axis=1)
    arrived = swap(sent, DEPTH)
    arrived, qkv_block, in_scale, head_gate, cosine, sine, residual, inside = (
        lax.optimization_barrier(
            (arrived, qkv_block, in_scale, head_gate, cosine, sine, residual, inside)
        )
    )
    batch = arrived[:, :rows].reshape(Z * rows, Y * depth)
    out_block = (
        arrived[:, 8:].reshape(Z, 2, -1, head_dim).transpose(1, 0, 2, 3).reshape(2, -1, head_dim)
    )
    part = jnp.dot(batch, qkv_block, preferred_element_type=F32).astype(BF16)
    part, out_block = lax.optimization_barrier((part.reshape(Z, rows, columns), out_block))
    part = swap(part, DEPTH)
    qkv = jnp.sum(part.astype(F32), axis=0) * in_scale
    query = qkv[:, : 2 * head_dim].reshape(rows, 2, head_dim)
    query = rotate(rms_scale(query, q_gain[0]), cosine[:, None], sine[:, None]).astype(BF16)
    key = qkv[:, 2 * head_dim : 3 * head_dim]
    key = rotate(rms_scale(key, k_gain[0]), cosine, sine).astype(BF16)
    value = qkv[:, 3 * head_dim :].astype(BF16)
    scale = head_dim ** (-0.5)
    keys, values = (kv_cache[0, 0, :, 0], kv_cache[0, 1, :, 0])
    score = jnp.einsum("rqd,sd->rqs", query, keys, preferred_element_type=F32) * scale
    weight = jnp.where(inside[:, None, :], jnp.exp(score), 0.0)
    own = jnp.exp(jnp.sum(query.astype(F32) * key.astype(F32)[:, None], axis=-1) * scale)
    total = jnp.sum(weight, axis=-1) + own
    summed = jnp.einsum("rqs,sd->rqd", weight.astype(BF16), values, preferred_element_type=F32)
    summed = summed + own.astype(BF16).astype(F32)[..., None] * value.astype(F32)[:, None]
    attended = summed / total[..., None]
    mixed = (attended * head_gate[..., None]).astype(BF16)
    everyone = spread(mixed.transpose(1, 0, 2).reshape(2 * rows, head_dim), "y", Y).reshape(
        Y, 2, rows, head_dim
    )
    part = jnp.einsum("yqrd,qnd->yrn", everyone, out_block, preferred_element_type=F32)
    part = swap(part.reshape(Y * rows * C, 2, head_dim), ("y", "x", "c"))
    projected = jnp.sum(part.reshape(Y, X * C, 2, head_dim), axis=1).reshape(8, head_dim)
    stream = (residual.astype(F32) + projected).astype(BF16)
    stream, post_gain = lax.optimization_barrier((stream, post_gain))
    post_half = own_core(post_gain.reshape(X, C, seg), 1).reshape(X, seg)
    gate_up = ffn[:, :, : 2 * units].transpose(1, 0, 2, 3)
    down = ffn[:, :, 2 * units :]
    batch, gate_up, down, post_half = lax.optimization_barrier(
        (spread(stream, DEPTH, Z), gate_up, down, post_half)
    )
    batch = batch.reshape(Z, X, seg)
    wide = batch.astype(F32)
    squares = jnp.sum(wide * wide, axis=(1, 2)).reshape(Z, 1)
    batch = (wide * post_half).astype(BF16)
    part = jnp.einsum("bxk,xyfk->byf", batch, gate_up, preferred_element_type=F32)
    part = jnp.concatenate([part.reshape(Z, -1), jnp.broadcast_to(squares, (Z, head_dim))], axis=1)
    both = jnp.sum(lax.all_gather(part, "c", axis=0), axis=0)
    scale = lax.rsqrt(both[:, -1:] / width + EPSILON)
    both = (both[:, :-head_dim] * scale).reshape(Z, Y, 2 * units)
    hidden = (jax.nn.silu(both[..., :units]) * both[..., units:]).astype(BF16)
    part = jnp.einsum("byf,yxfk->bxk", hidden, down, preferred_element_type=F32).astype(BF16)
    part = jnp.sum(spread(part.reshape(Z, 8, head_dim), "zl", ZL).astype(F32), axis=0).astype(BF16)
    lowered = jnp.sum(spread(part, "zh", ZH).astype(F32), axis=0)
    piece = (wide.reshape(Z, 8, head_dim) + lowered).astype(BF16).reshape(Z, part_width)
    near = spread(piece, ("y", "x"), Y * X).reshape(Y * X * Z, part_width)
    far = lax.ppermute(near, "c", [(0, 1), (1, 0)])
    near, far = (near.astype(F32), far.astype(F32))
    mean_square = (
        jnp.sum(near * near, axis=-1, keepdims=True) + jnp.sum(far * far, axis=-1, keepdims=True)
    ) / width
    scale = lax.rsqrt(mean_square + EPSILON)

    def scored(half, core):
        gain = lax.dynamic_slice_in_dim(final_gain.reshape(X, C, seg), core, 1, 1).reshape(
            1, part_width
        )
        vocab = lax.dynamic_slice_in_dim(w_vocab.reshape(X, C, seg, -1), core, 1, 1).reshape(
            part_width, -1
        )
        return jnp.dot((half * scale * gain).astype(BF16), vocab, preferred_element_type=F32)

    logits = (scored(near, ic) + scored(far, 1 - ic)).astype(BF16)
    logits = logits.reshape(Y, X, Z, w_vocab.shape[1]).transpose(0, 2, 1, 3)
    return logits.reshape(Y * X * Z, w_vocab.shape[1])


def solution(mesh):
    fine = Mesh(mesh.devices.reshape(Y, ZH, ZL, X, C), ("y", "zh", "zl", "x", "c"))
    req, head = (("y",) + DEPTH, ("x", "c"))
    in_specs = (
        P(req, None),
        P(),
        P(None, None, req, head, None),
        P(None, req, head, None),
        P(None, None, head),
        P(None, head, req),
        P(),
        P(),
        P(),
        P(),
        P(None, head, req),
        P(None, head, req),
        P(None, req, head),
        P(),
        P(None, req + head),
    )
    out_specs = P(None, req + head)
    return jax.shard_map(local, mesh=fine, in_specs=in_specs, out_specs=out_specs, check_vma=False)
```

profile of v0, /device:TPU:1, one launch (start us, length us, event | category | flops | bytes accessed | tf_op | source)
XLA Modules:
  0.0 161.6 jit_solution(16570574454729380939)
XLA Ops:
  6.6 0.8 fusion.47
  7.4 0.8 fusion.26
  8.6 0.8 pad_maximum_fusion
  9.5 15.9 %all-to-all-start = ((bf16[16,72,128]{2,1,0:T(8,128)(2,1)}), bf16[16,72,128]{2,1,0:T(8,128)(2,1)S(1)}, u32[]{:S(2)}, u32[]{:S(2)}) async-start(bf16[16,72,128]{2,1,0:T(8,128)(2,1)} %pad_maximum_fusion), calls=%async_computation | async-start | bytes 589824 | tf_op jit(solution)/shard_map/all_to_all | solution.py:27
  25.4 0.7 pad_maximum_fusion.1
  26.8 10.4 %all-gather = bf16[1,128,1,512]{3,1,2,0:T(8,128)(2,1)S(1)} all-gather(bf16[1,32,1,512]{3,1,2,0:T(8,128)(2,1)S(1)} %copy-done.6), channel_id=2, replica_groups=mesh['y'=4,'zh'=4,'zl'=4,'x'=4,'c'=2] {'y'}, dimensions={1}, use_global_device_ids=true | all-gather | bytes 163840 | tf_op jit(solution)/shard_map/all_gather | solution.py:61
  37.2 0.2 fusion.10
  37.4 1.7 %all-to-all-done = bf16[16,72,128]{2,1,0:T(8,128)(2,1)S(1)} async-done(((bf16[16,72,128]{2,1,0:T(8,128)(2,1)}), bf16[16,72,128]{2,1,0:T(8,128)(2,1)S(1)}, u32[]{:S(2)}, u32[]{:S(2)}) %all-to-all-start) | async-done | bytes 294944 | tf_op jit(solution)/shard_map/all_to_all | solution.py:27
  39.4 23.1 %all_to_all.40 = bf16[16,4,512]{2,1,0:T(4,128)(2,1)S(1)} all-to-all(bf16[16,4,512]{2,1,0:T(4,128)(2,1)S(1)} %reshape.228), channel_id=1, replica_groups=mesh['y'=4,'zh'=4,'zl'=4,'x'=4,'c'=2] {'zh','zl'}, dimensions={0} | all-to-all | bytes 131072 | tf_op jit(solution)/shard_map/all_to_all | solution.py:27
  63.3 0.3 fusion.48
  63.8 8.2 %all_to_all.41 = bf16[4,8,128]{2,1,0:T(8,128)(2,1)S(1)} all-to-all(bf16[4,8,128]{2,1,0:T(8,128)(2,1)S(1)} %broadcast_in_dim.42), channel_id=1, replica_groups=mesh['y'=4,'zh'=4,'zl'=4,'x'=4,'c'=2] {'y'}, dimensions={0} | all-to-all | bytes 16384 | tf_op jit(solution)/shard_map/all_to_all | solution.py:27
  72.2 15.9 %all_to_all.42 = f32[32,2,128]{2,1,0:T(2,128)S(1)} all-to-all(f32[32,2,128]{2,1,0:T(2,128)S(1)} %reshape.233), channel_id=1, replica_groups=mesh['y'=4,'zh'=4,'zl'=4,'x'=4,'c'=2] {'y','x','c'}, dimensions={0} | all-to-all | bytes 65536 | tf_op jit(solution)/shard_map/all_to_all | solution.py:27
  88.2 0.6 broadcast_in_dim.43
  88.8 3.5 %all-to-all-start.4 = ((bf16[16,8,128]{2,1,0:T(8,128)(2,1)}), bf16[16,8,128]{2,1,0:T(8,128)(2,1)S(1)}, u32[]{:S(2)}, u32[]{:S(2)}) async-start(bf16[16,8,128]{2,1,0:T(8,128)(2,1)} %broadcast_in_dim.43), calls=%async_computation.4 | async-start | bytes 65536 | tf_op jit(solution)/shard_map/all_to_all | solution.py:27
  92.3 0.5 broadcast.164
  92.8 0.6 reduce.12
  93.5 1.5 slice_bitcast_fusion
  95.0 1.2 slice.85
  96.3 7.5 %all-to-all-done.4 = bf16[16,8,128]{2,1,0:T(8,128)(2,1)S(1)} async-done(((bf16[16,8,128]{2,1,0:T(8,128)(2,1)}), bf16[16,8,128]{2,1,0:T(8,128)(2,1)S(1)}, u32[]{:S(2)}, u32[]{:S(2)}) %all-to-all-start.4) | async-done | bytes 32800 | tf_op jit(solution)/shard_map/all_to_all | solution.py:27
  103.8 0.2 multiply_reduce_fusion
  104.2 0.5 convolution_bitcast_fusion.1
  104.8 2.9 %all-gather.2 = f32[32,896]{1,0:T(8,128)S(1)} all-gather(f32[16,896]{1,0:T(8,128)S(1)} %pad_maximum_fusion.2), channel_id=4, replica_groups=mesh['y'=4,'zh'=4,'zl'=4,'x'=4,'c'=2] {'c'}, dimensions={0}, use_global_device_ids=true | all-gather | bytes 172032 | tf_op jit(solution)/shard_map/all_gather | solution.py:143
  108.2 0.3 fusion.1
  108.5 7.4 %all_to_all.43 = bf16[4,16,8,128]{3,2,1,0:T(8,128)(2,1)S(1)} all-to-all(bf16[4,16,8,128]{3,2,1,0:T(8,128)(2,1)S(1)} %broadcast_in_dim.46), channel_id=1, replica_groups=mesh['y'=4,'zh'=4,'zl'=4,'x'=4,'c'=2] {'zl'}, dimensions={0} | all-to-all | bytes 262144 | tf_op jit(solution)/shard_map/all_to_all | solution.py:27
  116.0 15.6 %all_to_all.44 = bf16[4,16,8,128]{3,2,1,0:T(8,128)(2,1)S(1)} all-to-all(bf16[4,16,8,128]{3,2,1,0:T(8,128)(2,1)S(1)} %broadcast_in_dim.47), channel_id=1, replica_groups=mesh['y'=4,'zh'=4,'zl'=4,'x'=4,'c'=2] {'zh'}, dimensions={0} | all-to-all | bytes 262144 | tf_op jit(solution)/shard_map/all_to_all | solution.py:27
  131.7 11.8 %all_to_all.45 = bf16[16,16,1024]{2,1,0:T(8,128)(2,1)S(1)} all-to-all(bf16[16,16,1024]{2,1,0:T(8,128)(2,1)S(1)} %broadcast_in_dim.49), channel_id=1, replica_groups=mesh['y'=4,'zh'=4,'zl'=4,'x'=4,'c'=2] {'y','x'}, dimensions={0} | all-to-all | bytes 1048576 | tf_op jit(solution)/shard_map/all_to_all | solution.py:27
  143.5 7.9 %collective-permute-start = (bf16[256,1024]{1,0:T(8,128)(2,1)S(1)}, bf16[256,1024]{1,0:T(8,128)(2,1)S(1)}, u32[]{:S(2)}, u32[]{:S(2)}) collective-permute-start(bf16[256,1024]{1,0:T(8,128)(2,1)S(1)} %bitcast.122), channel_id=1, source_target_pairs={{0,1},{1,0},{2,3},{3,2},{4,5},{5,4},{6,7},{7,6},{8,9},{9,8},{10,11... | collective-permute-start | bytes 1572872 | tf_op jit(solution)/shard_map/ppermute | solution.py:152
  151.7 1.1 collective-permute-done
  153.1 0.2 fusion.13
  153.3 0.3 fusion.49
  153.7 0.4 fusion
  154.1 0.7 reshape.246
  (108 shorter events, 4.3 us)
Async XLA Ops:
  6.5 30.6 %copy-start = (bf16[1,2048,2]{1,2,0:T(2,128)(2,1)S(1)}, bf16[1,2048,2]{1,2,0:T(2,128)(2,1)}, u32[]{:S(2)}) copy-start(bf16[1,2048,2]{1,2,0:T(2,128)(2,1)} %param.19) | copy-start | bytes 24580
  6.5 20.2 %copy-start.5 = (bf16[4,2048]{1,0:T(4,128)(2,1)S(1)}, bf16[4,2048]{1,0:T(4,128)(2,1)}, u32[]{:S(2)}) copy-start(bf16[4,2048]{1,0:T(4,128)(2,1)} %param.15) | copy-start | bytes 49156
  6.5 30.6 %copy-start.9 = (f32[1,2048]{1,0:T(1,128)S(1)}, f32[1,2048]{1,0:T(1,128)}, u32[]{:S(2)}) copy-start(f32[1,2048]{1,0:T(1,128)} %param.21) | copy-start | bytes 24580
  6.5 18.9 %copy-start.2 = (bf16[1,96,256]{2,1,0:T(8,128)(2,1)S(1)}, bf16[1,96,256]{2,1,0:T(8,128)(2,1)}, u32[]{:S(2)}) copy-start(bf16[1,96,256]{2,1,0:T(8,128)(2,1)} %param.27) | copy-start | bytes 147460
  6.5 18.9 %copy-start.3 = (bf16[1,256,96]{1,2,0:T(8,128)(2,1)S(1)}, bf16[1,256,96]{1,2,0:T(8,128)(2,1)}, u32[]{:S(2)}) copy-start(bf16[1,256,96]{1,2,0:T(8,128)(2,1)} %param.26) | copy-start | bytes 147460
  6.5 18.9 %copy-start.4 = (bf16[1,256,96]{1,2,0:T(8,128)(2,1)S(1)}, bf16[1,256,96]{1,2,0:T(8,128)(2,1)}, u32[]{:S(2)}) copy-start(bf16[1,256,96]{1,2,0:T(8,128)(2,1)} %param.25) | copy-start | bytes 147460
  6.6 19.6 %copy-start.12 = (s32[256]{0:T(256)S(1)}, s32[256]{0:T(256)}, u32[]{:S(2)}) copy-start(s32[256]{0:T(256)} %param.16) | copy-start | bytes 3076
  6.6 20.3 %copy-start.6 = (bf16[1,32,1,512]{3,1,2,0:T(8,128)(2,1)S(1)}, bf16[1,32,1,512]{3,1,2,0:T(8,128)(2,1)}, u32[]{:S(2)}) copy-start(bf16[1,32,1,512]{3,1,2,0:T(8,128)(2,1)} %param.18) | copy-start | bytes 98308
  9.5 53.2 %copy-start.10 = (f32[1,128]{1,0:T(1,128)S(1)}, f32[1,128]{1,0:T(1,128)}, u32[]{:S(2)}) copy-start(f32[1,128]{1,0:T(1,128)} %param.23) | copy-start | bytes 1540
  9.5 53.5 %copy-start.11 = (f32[1,128]{1,0:T(1,128)S(1)}, f32[1,128]{1,0:T(1,128)}, u32[]{:S(2)}) copy-start(f32[1,128]{1,0:T(1,128)} %param.22) | copy-start | bytes 1540
  9.5 53.8 %copy-start.13 = (bf16[1,2,1024,1,128]{4,2,3,1,0:T(8,128)(2,1)S(1)}, bf16[1,2,1024,1,128]{4,2,3,1,0:T(8,128)(2,1)}, u32[]{:S(2)}) copy-start(bf16[1,2,1024,1,128]{4,2,3,1,0:T(8,128)(2,1)} %param.17) | copy-start | bytes 1572868
  9.5 29.6 %all-to-all-start = ((bf16[16,72,128]{2,1,0:T(8,128)(2,1)}), bf16[16,72,128]{2,1,0:T(8,128)(2,1)S(1)}, u32[]{:S(2)}, u32[]{:S(2)}) async-start(bf16[16,72,128]{2,1,0:T(8,128)(2,1)} %pad_maximum_fusion), calls=%async_computation | async-start | bytes 589824 | tf_op jit(solution)/shard_map/all_to_all | solution.py:27
  25.4 68.1 %all-gather.5.cloned.1.call-start = ((), (), s32[]{:S(2)}) async-start(), calls=%async_computation.8 | async-start | bytes 2506752 | tf_op jit(solution)/shard_map/all_gather | solution.py:60
  37.4 55.4 %copy-start.7 = (f32[1,2048]{1,0:T(1,128)S(1)}, f32[1,2048]{1,0:T(1,128)}, u32[]{:S(2)}) copy-start(f32[1,2048]{1,0:T(1,128)} %param.24) | copy-start | bytes 24580
  88.8 15.0 %all-to-all-start.4 = ((bf16[16,8,128]{2,1,0:T(8,128)(2,1)}), bf16[16,8,128]{2,1,0:T(8,128)(2,1)S(1)}, u32[]{:S(2)}, u32[]{:S(2)}) async-start(bf16[16,8,128]{2,1,0:T(8,128)(2,1)} %broadcast_in_dim.43), calls=%async_computation.4 | async-start | bytes 65536 | tf_op jit(solution)/shard_map/all_to_all | solution.py:27
  108.4 42.9 %copy-start.8 = (f32[2048]{0:T(1024)S(1)}, f32[2048]{0:T(1024)}, u32[]{:S(2)}) copy-start(f32[2048]{0:T(1024)} %param.28) | copy-start | bytes 24580
  108.5 42.9 %copy-start.1 = (bf16[2048,256]{1,0:T(8,128)(2,1)S(1)}, bf16[2048,256]{1,0:T(8,128)(2,1)}, u32[]{:S(2)}) copy-start(bf16[2048,256]{1,0:T(8,128)(2,1)} %param.29) | copy-start | bytes 3145732
  143.5 9.4 %collective-permute-start = (bf16[256,1024]{1,0:T(8,128)(2,1)S(1)}, bf16[256,1024]{1,0:T(8,128)(2,1)S(1)}, u32[]{:S(2)}, u32[]{:S(2)}) collective-permute-start(bf16[256,1024]{1,0:T(8,128)(2,1)S(1)} %bitcast.122), channel_id=1, source_target_pairs={{0,1},{1,0},{2,3},{3,2},{4,5},{5,4},{6,7},{7,6},{8,9},{9,8},{10,11... | collective-permute-start | bytes 1572872 | tf_op jit(solution)/shard_map/ppermute | solution.py:152
Sparse Core Ops, SparseCore 0:
  29.2 61.6 all-gather.4
where the time goes:
time: 162 us
  blocking collectives  95.2 us (59%)
  starting transfers between devices  27.3 us (17%)
  between operations  13.9 us (9%)
  waiting for transfers between devices  10.4 us (6%)
  local copies, waits for them, and re-layouts  6.97 us (4%)
  other arithmetic  5.44 us (3%)
  matrix products  2.44 us (2%)
    all_to_all x6, blocking collectives, swap(): return lax.all_to_all(values, axes, split_axis=0, concat_axis=0, tiled=True)  82 us
    all_to_all x2, starting transfers between devices, swap(): return lax.all_to_all(values, axes, split_axis=0, concat_axis=0, tiled=True)  19.4 us
    all_gather x1, blocking collectives, local(): qkv_block = lax.all_gather(w_qkv[0, :, 0], 'y', axis=0, tiled=True)  10.4 us
    all_to_all x2, waiting for transfers between devices, swap(): return lax.all_to_all(values, axes, split_axis=0, concat_axis=0, tiled=True)  9.26 us
    ppermute x1, starting transfers between devices, local(): far = lax.ppermute(near, 'c', [(0, 1), (1, 0)])  7.85 us
  transfers between devices with their start and end apart: 4, of which 3 were waited for; matrix products, arithmetic and copies ran while one was open for 5% of the time, Pallas kernels for 0%

commit v1 on v0

--- a/solution.py
+++ b/solution.py
@@ -58,7 +58,9 @@
     ix, ic = (lax.axis_index("x"), lax.axis_index("c"))
     ffn = jnp.concatenate([w_gate[0].T, w_up[0].T, w_down[0]], axis=0)
     ffn = lax.all_gather(ffn, ("y", "x"), axis=0).reshape(Y, X, -1, seg)
-    qkv_block = lax.all_gather(w_qkv[0, :, 0], "y", axis=0, tiled=True)
+    qkv_block = jnp.concatenate(
+        lax.all_to_all(jnp.stack([w_qkv[0, :, 0]] * lax.axis_size("y")), "y", 0, 0), axis=0
+    )
     positions = lax.dynamic_slice_in_dim(lengths, req * rows, rows)
     starts = jnp.cumsum(positions) - positions
     limits = starts + positions

time: 162 us -> 170 us (1.049)
  waiting for transfers between devices: 10.4 us -> 21.2 us
  blocking collectives: 95.2 us -> 85.3 us
  starting transfers between devices: 27.3 us -> 31.3 us
  local copies, waits for them, and re-layouts: 6.97 us -> 9.04 us
    all_to_all x2, waiting for transfers between devices: 9.26 us -> 20.1 us  [swap(): return lax.all_to_all(values, axes, split_axis=0, concat_axis=0, tiled=True)]
    all_gather x1 -> x0, blocking collectives: 10.4 us -> none  [local(): qkv_block = lax.all_gather(w_qkv[0, :, 0], 'y', axis=0, tiled=True)]
    all_to_all x0 -> x1, starting transfers between devices: none -> 5.01 us  [local(): lax.all_to_all(jnp.stack([w_qkv[0, :, 0]] * lax.axis_size('y')), 'y', 0, 0)]
    another operation x1 -> x2, local copies, waits for them, and re-layouts: 0.08 us -> 2.22 us  [the longest x1 1.46 us: local(): jnp.stack([w_qkv[0, :, 0]] * lax.axis_size('y'))]
  transfers between devices with their start and end apart: 4 -> 5, of which waited for: 3 -> 3; matrix products, arithmetic and copies ran while one was open for 5% -> 7% of each run, Pallas kernels for 0% -> 0%
where the time goes in v1:
time: 170 us; the launch traced here: 169 us
  blocking collectives  85.3 us (50%)
  starting transfers between devices  31.3 us (18%)
  waiting for transfers between devices  21.2 us (12%)
  between operations  13.8 us (8%)
  local copies, waits for them, and re-layouts  9.04 us (5%)
  other arithmetic  6.29 us (4%)
  matrix products  2.45 us (1%)
    all_to_all x6, blocking collectives, swap(): return lax.all_to_all(values, axes, split_axis=0, concat_axis=0, tiled=True)  82.4 us
    all_to_all x2, waiting for transfers between devices, swap(): return lax.all_to_all(values, axes, split_axis=0, concat_axis=0, tiled=True)  20.1 us
    all_to_all x2, starting transfers between devices, swap(): return lax.all_to_all(values, axes, split_axis=0, concat_axis=0, tiled=True)  18.4 us
    ppermute x1, starting transfers between devices, local(): far = lax.ppermute(near, 'c', [(0, 1), (1, 0)])  7.88 us
    all_to_all x1, starting transfers between devices, local(): lax.all_to_all(jnp.stack([w_qkv[0, :, 0]] * lax.axis_size('y')), 'y', 0, 0)  5.01 us
  transfers between devices with their start and end apart: 5, of which 3 were waited for; matrix products, arithmetic and copies ran while one was open for 7% of the time, Pallas kernels for 0%

profile of v1, /device:TPU:1, one launch (start us, length us, event | category | flops | bytes accessed | tf_op | source)
XLA Modules:
  0.0 169.4 jit_solution(398655541406828810)
XLA Ops:
  6.5 1.5 stack.3
  8.0 5.0 %all-to-all-start.1 = ((bf16[4,32,512]{2,1,0:T(8,128)(2,1)}), bf16[4,32,512]{2,1,0:T(8,128)(2,1)S(1)}, u32[]{:S(2)}, u32[]{:S(2)}) async-start(bf16[4,32,512]{2,1,0:T(8,128)(2,1)} %stack.3), calls=%async_computation.1 | async-start | bytes 262144 | tf_op jit(solution)/shard_map/all_to_all | solution.py:62
  13.0 1.5 pad_maximum_fusion.1
  14.6 0.7 fusion.47
  15.3 0.8 fusion.26
  16.4 0.8 dynamic-slice_bitcast_fusion
  17.5 0.8 pad_maximum_fusion
  18.4 14.9 %all-to-all-start = ((bf16[16,72,128]{2,1,0:T(8,128)(2,1)}), bf16[16,72,128]{2,1,0:T(8,128)(2,1)S(1)}, u32[]{:S(2)}, u32[]{:S(2)}) async-start(bf16[16,72,128]{2,1,0:T(8,128)(2,1)} %pad_maximum_fusion), calls=%async_computation | async-start | bytes 589824 | tf_op jit(solution)/shard_map/all_to_all | solution.py:27
  33.9 12.5 %all-to-all-done = bf16[16,72,128]{2,1,0:T(8,128)(2,1)S(1)} async-done(((bf16[16,72,128]{2,1,0:T(8,128)(2,1)}), bf16[16,72,128]{2,1,0:T(8,128)(2,1)S(1)}, u32[]{:S(2)}, u32[]{:S(2)}) %all-to-all-start) | async-done | bytes 294944 | tf_op jit(solution)/shard_map/all_to_all | solution.py:27
  46.7 23.3 %all_to_all.45 = bf16[16,4,512]{2,1,0:T(4,128)(2,1)S(1)} all-to-all(bf16[16,4,512]{2,1,0:T(4,128)(2,1)S(1)} %reshape.234), channel_id=1, replica_groups=mesh['y'=4,'zh'=4,'zl'=4,'x'=4,'c'=2] {'zh','zl'}, dimensions={0} | all-to-all | bytes 131072 | tf_op jit(solution)/shard_map/all_to_all | solution.py:27
  70.9 0.3 fusion.48
  71.4 8.7 %all_to_all.46 = bf16[4,8,128]{2,1,0:T(8,128)(2,1)S(1)} all-to-all(bf16[4,8,128]{2,1,0:T(8,128)(2,1)S(1)} %broadcast_in_dim.42), channel_id=1, replica_groups=mesh['y'=4,'zh'=4,'zl'=4,'x'=4,'c'=2] {'y'}, dimensions={0} | all-to-all | bytes 16384 | tf_op jit(solution)/shard_map/all_to_all | solution.py:27
  80.4 15.6 %all_to_all.47 = f32[32,2,128]{2,1,0:T(2,128)S(1)} all-to-all(f32[32,2,128]{2,1,0:T(2,128)S(1)} %reshape.239), channel_id=1, replica_groups=mesh['y'=4,'zh'=4,'zl'=4,'x'=4,'c'=2] {'y','x','c'}, dimensions={0} | all-to-all | bytes 65536 | tf_op jit(solution)/shard_map/all_to_all | solution.py:27
  96.0 0.6 broadcast_in_dim.43
  96.6 3.5 %all-to-all-start.5 = ((bf16[16,8,128]{2,1,0:T(8,128)(2,1)}), bf16[16,8,128]{2,1,0:T(8,128)(2,1)S(1)}, u32[]{:S(2)}, u32[]{:S(2)}) async-start(bf16[16,8,128]{2,1,0:T(8,128)(2,1)} %broadcast_in_dim.43), calls=%async_computation.5 | async-start | bytes 65536 | tf_op jit(solution)/shard_map/all_to_all | solution.py:27
  100.1 0.5 broadcast.165
  100.7 0.6 reduce.12
  101.3 1.5 slice_bitcast_fusion
  102.8 1.2 slice.85
  104.1 7.5 %all-to-all-done.5 = bf16[16,8,128]{2,1,0:T(8,128)(2,1)S(1)} async-done(((bf16[16,8,128]{2,1,0:T(8,128)(2,1)}), bf16[16,8,128]{2,1,0:T(8,128)(2,1)S(1)}, u32[]{:S(2)}, u32[]{:S(2)}) %all-to-all-start.5) | async-done | bytes 32800 | tf_op jit(solution)/shard_map/all_to_all | solution.py:27
  111.6 0.2 multiply_reduce_fusion
  112.0 0.5 convolution_bitcast_fusion.1
  112.6 2.9 %all-gather.1 = f32[32,896]{1,0:T(8,128)S(1)} all-gather(f32[16,896]{1,0:T(8,128)S(1)} %pad_maximum_fusion.2), channel_id=3, replica_groups=mesh['y'=4,'zh'=4,'zl'=4,'x'=4,'c'=2] {'c'}, dimensions={0}, use_global_device_ids=true | all-gather | bytes 172032 | tf_op jit(solution)/shard_map/all_gather | solution.py:145
  116.0 0.3 fusion.1
  116.3 7.4 %all_to_all.48 = bf16[4,16,8,128]{3,2,1,0:T(8,128)(2,1)S(1)} all-to-all(bf16[4,16,8,128]{3,2,1,0:T(8,128)(2,1)S(1)} %broadcast_in_dim.46), channel_id=1, replica_groups=mesh['y'=4,'zh'=4,'zl'=4,'x'=4,'c'=2] {'zl'}, dimensions={0} | all-to-all | bytes 262144 | tf_op jit(solution)/shard_map/all_to_all | solution.py:27
  123.8 15.6 %all_to_all.49 = bf16[4,16,8,128]{3,2,1,0:T(8,128)(2,1)S(1)} all-to-all(bf16[4,16,8,128]{3,2,1,0:T(8,128)(2,1)S(1)} %broadcast_in_dim.47), channel_id=1, replica_groups=mesh['y'=4,'zh'=4,'zl'=4,'x'=4,'c'=2] {'zh'}, dimensions={0} | all-to-all | bytes 262144 | tf_op jit(solution)/shard_map/all_to_all | solution.py:27
  139.5 11.8 %all_to_all.50 = bf16[16,16,1024]{2,1,0:T(8,128)(2,1)S(1)} all-to-all(bf16[16,16,1024]{2,1,0:T(8,128)(2,1)S(1)} %broadcast_in_dim.49), channel_id=1, replica_groups=mesh['y'=4,'zh'=4,'zl'=4,'x'=4,'c'=2] {'y','x'}, dimensions={0} | all-to-all | bytes 1048576 | tf_op jit(solution)/shard_map/all_to_all | solution.py:27
  151.2 7.9 %collective-permute-start = (bf16[256,1024]{1,0:T(8,128)(2,1)S(1)}, bf16[256,1024]{1,0:T(8,128)(2,1)S(1)}, u32[]{:S(2)}, u32[]{:S(2)}) collective-permute-start(bf16[256,1024]{1,0:T(8,128)(2,1)S(1)} %bitcast.123), channel_id=1, source_target_pairs={{0,1},{1,0},{2,3},{3,2},{4,5},{5,4},{6,7},{7,6},{8,9},{9,8},{10,11... | collective-permute-start | bytes 1572872 | tf_op jit(solution)/shard_map/ppermute | solution.py:154
  159.5 1.1 collective-permute-done
  161.1 0.3 fusion.49
  161.4 0.4 fusion
  161.9 0.7 reshape.252
  (102 shorter events, 4.6 us)
Async XLA Ops:
  6.5 27.2 %copy-start = (bf16[1,2048,2]{1,2,0:T(2,128)(2,1)S(1)}, bf16[1,2048,2]{1,2,0:T(2,128)(2,1)}, u32[]{:S(2)}) copy-start(bf16[1,2048,2]{1,2,0:T(2,128)(2,1)} %param.19) | copy-start | bytes 24580
  6.5 27.1 %copy-start.2 = (bf16[4,2048]{1,0:T(4,128)(2,1)S(1)}, bf16[4,2048]{1,0:T(4,128)(2,1)}, u32[]{:S(2)}) copy-start(bf16[4,2048]{1,0:T(4,128)(2,1)} %param.15) | copy-start | bytes 49156
  6.5 27.2 %copy-start.5 = (f32[1,2048]{1,0:T(1,128)S(1)}, f32[1,2048]{1,0:T(1,128)}, u32[]{:S(2)}) copy-start(f32[1,2048]{1,0:T(1,128)} %param.21) | copy-start | bytes 24580
  6.5 26.8 %copy-start.8 = (s32[256]{0:T(256)S(1)}, s32[256]{0:T(256)}, u32[]{:S(2)}) copy-start(s32[256]{0:T(256)} %param.16) | copy-start | bytes 3076
  8.0 10.4 %all-to-all-start.1 = ((bf16[4,32,512]{2,1,0:T(8,128)(2,1)}), bf16[4,32,512]{2,1,0:T(8,128)(2,1)S(1)}, u32[]{:S(2)}, u32[]{:S(2)}) async-start(bf16[4,32,512]{2,1,0:T(8,128)(2,1)} %stack.3), calls=%async_computation.1 | async-start | bytes 262144 | tf_op jit(solution)/shard_map/all_to_all | solution.py:62
  13.0 88.3 %all-gather.4.cloned.1.call-start = ((), (), s32[]{:S(2)}) async-start(), calls=%async_computation.9 | async-start | bytes 2506752 | tf_op jit(solution)/shard_map/all_gather | solution.py:60
  17.4 52.8 %copy-start.6 = (f32[1,128]{1,0:T(1,128)S(1)}, f32[1,128]{1,0:T(1,128)}, u32[]{:S(2)}) copy-start(f32[1,128]{1,0:T(1,128)} %param.23) | copy-start | bytes 1540
  17.5 53.1 %copy-start.7 = (f32[1,128]{1,0:T(1,128)S(1)}, f32[1,128]{1,0:T(1,128)}, u32[]{:S(2)}) copy-start(f32[1,128]{1,0:T(1,128)} %param.22) | copy-start | bytes 1540
  17.5 53.4 %copy-start.9 = (bf16[1,2,1024,1,128]{4,2,3,1,0:T(8,128)(2,1)S(1)}, bf16[1,2,1024,1,128]{4,2,3,1,0:T(8,128)(2,1)}, u32[]{:S(2)}) copy-start(bf16[1,2,1024,1,128]{4,2,3,1,0:T(8,128)(2,1)} %param.17) | copy-start | bytes 1572868
  18.4 28.1 %all-to-all-start = ((bf16[16,72,128]{2,1,0:T(8,128)(2,1)}), bf16[16,72,128]{2,1,0:T(8,128)(2,1)S(1)}, u32[]{:S(2)}, u32[]{:S(2)}) async-start(bf16[16,72,128]{2,1,0:T(8,128)(2,1)} %pad_maximum_fusion), calls=%async_computation | async-start | bytes 589824 | tf_op jit(solution)/shard_map/all_to_all | solution.py:27
  33.9 66.7 %copy-start.3 = (f32[1,2048]{1,0:T(1,128)S(1)}, f32[1,2048]{1,0:T(1,128)}, u32[]{:S(2)}) copy-start(f32[1,2048]{1,0:T(1,128)} %param.24) | copy-start | bytes 24580
  96.6 15.0 %all-to-all-start.5 = ((bf16[16,8,128]{2,1,0:T(8,128)(2,1)}), bf16[16,8,128]{2,1,0:T(8,128)(2,1)S(1)}, u32[]{:S(2)}, u32[]{:S(2)}) async-start(bf16[16,8,128]{2,1,0:T(8,128)(2,1)} %broadcast_in_dim.43), calls=%async_computation.5 | async-start | bytes 65536 | tf_op jit(solution)/shard_map/all_to_all | solution.py:27
  116.2 42.9 %copy-start.4 = (f32[2048]{0:T(1024)S(1)}, f32[2048]{0:T(1024)}, u32[]{:S(2)}) copy-start(f32[2048]{0:T(1024)} %param.28) | copy-start | bytes 24580
  116.3 42.9 %copy-start.1 = (bf16[2048,256]{1,0:T(8,128)(2,1)S(1)}, bf16[2048,256]{1,0:T(8,128)(2,1)}, u32[]{:S(2)}) copy-start(bf16[2048,256]{1,0:T(8,128)(2,1)} %param.29) | copy-start | bytes 3145732
  151.2 9.4 %collective-permute-start = (bf16[256,1024]{1,0:T(8,128)(2,1)S(1)}, bf16[256,1024]{1,0:T(8,128)(2,1)S(1)}, u32[]{:S(2)}, u32[]{:S(2)}) collective-permute-start(bf16[256,1024]{1,0:T(8,128)(2,1)S(1)} %bitcast.123), channel_id=1, source_target_pairs={{0,1},{1,0},{2,3},{3,2},{4,5},{5,4},{6,7},{7,6},{8,9},{9,8},{10,11... | collective-permute-start | bytes 1572872 | tf_op jit(solution)/shard_map/ppermute | solution.py:154
Sparse Core Ops, SparseCore 0:
  16.8 65.0 all-gather.3
